TPU v7x, 32 devices: a whole 2x2x4 slice. The times are simulated.
32 devices in a mesh: energy: 2 (over x), chain: 16 (over z, y, core).
Axes of the slice: x: 2, y: 2, z: 4, core: 2. Of those that a mesh axis runs over, the one named last changes fastest.
Arguments:
- lower: bfloat16 [32, 2, 256, 256], P(('energy', 'chain')), parts along dimension 0, may hold values from -0.125 to 0.125
- upper: bfloat16 [32, 2, 256, 256], P(('energy', 'chain')), parts along dimension 0, may hold values from -0.125 to 0.125
- right_side: bfloat16 [32, 2, 256, 256], P(('energy', 'chain')), parts along dimension 0, may hold values from -6 to 6
Outputs:
- reduced_rhs: bfloat16 [32, 2, 256, 256], P(('energy', 'chain')), parts along dimension 0
There are 2 independent parts, one for each index of `energy`. A program takes and returns all parts, laid end to end along the dimension named above; each array names one. Nothing has to cross between parts.
All inputs are finite; a program needn't handle non-finite values.
Results may differ from a plain program's by a relative error of at most 0.011.
Values may be sent and summed in bfloat16 or wider, within the bound.
A program may use at most 64 MiB of HBM per device.

v0:
```python
import functools

import jax
import jax.numpy as jnp
from jax import lax
from jax.experimental import pallas as pl
from jax.experimental.pallas import tpu as pltpu
from jax.sharding import PartitionSpec as P

NS_STEPS = 2
MESH = pl.DeviceIdType.MESH
RHS = 2


def is_rhs(u):
    return isinstance(u, int) and u >= RHS


def product(left, right):
    order = left.shape[1]
    tall = left.reshape(2 * order, left.shape[2])
    by_real = jnp.dot(tall, right[0], preferred_element_type=jnp.float32)
    by_imag = jnp.dot(tall, right[1], preferred_element_type=jnp.float32)
    return by_real[:order] - by_imag[order:], by_imag[:order] + by_real[order:]


def rounded(parts):
    return jnp.stack([parts[0].astype(jnp.bfloat16), parts[1].astype(jnp.bfloat16)])


def kernel(
    quads, l_ref, u_ref, b_ref, out_ref,
    buf, bbuf, new1, nb1, got1, gb1, new2, nb2, got2, gb2, last, mid, fwd,
    sem_home, sem_bhome, sem_buf, sem_send0, sem_relay,
    sem_got1, sem_send1, sem_got2, sem_send2, sem_out, sem_fwd,
):
    me = lax.axis_index("chain")
    q = me // 4
    a = (me // 2) % 2
    b = me % 2
    inner = a != b
    outer = a == b
    f = 1 - a
    g = a
    cf = 2 - a
    cg = 1 + a

    def at(quad, y, core):
        return {"chain": quad * 4 + y * 2 + core}

    mate = at(q, a, 1 - b)
    across = at(q, 1 - a, b)
    twin = at(q, b, a)
    up1, has_up1 = at(q + b, a, 1 - b), q + b < quads
    down1, has_down1 = at(q - 1 + b, a, 1 - b), q - 1 + b >= 0
    up2, has_up2 = at(q + 1, a, b), q + 1 < quads
    down2, has_down2 = at(q - 1, a, b), q >= 1
    far_step = 2 * b - 1
    far, has_far = at(q + far_step, a, 1 - b), (q + far_step >= 0) & (q + far_step < quads)
    diag = at(q, 1 - a, 1 - b)
    pass_on = {"chain": jnp.where(a == 0, down2["chain"], up2["chain"])}
    has_far_in = ((a == 0) & has_up2) | ((a == 1) & has_down2)
    has_pass_on = outer & (((a == 0) & has_down2) | ((a == 1) & has_up2))
    inputs = (l_ref, u_ref)
    wide = b_ref.shape[3] // 2

    def place0(slot, u, half):
        return bbuf.at[slot, half] if is_rhs(u) else buf.at[slot, u, half]

    home_slot = jnp.where(inner, 1 + a, 0)
    def load(u):
        return pltpu.make_async_copy(inputs[u].at[0], buf.at[home_slot, u], sem_home.at[u])

    def load_rhs(half, part):
        return pltpu.make_async_copy(
            b_ref.at[0, part, :, pl.ds(half * wide, wide)],
            bbuf.at[home_slot, half, :, pl.ds(part * wide, wide)],
            sem_bhome.at[half, part],
        )

    for u in (0, 1):
        load(u).start()
    for half in range(2):
        for part in range(2):
            load_rhs(half, part).start()

    barrier = pltpu.get_barrier_semaphore()

    def greet(who):
        pl.semaphore_signal(barrier, inc=1, device_id=who, device_id_type=MESH)

    greet(mate)
    greet(across)
    for exists, who in ((inner, twin), (outer, diag), (has_far, far), (has_up2, up2), (has_down2, down2)):
        pl.when(exists)(functools.partial(greet, who))
    count = (
        3
        + has_far.astype(jnp.int32)
        + has_up2.astype(jnp.int32)
        + has_down2.astype(jnp.int32)
    )
    pl.semaphore_wait(barrier, count)

    def remote(src, dst, send, recv, who):
        return pltpu.make_async_remote_copy(
            src_ref=src, dst_ref=dst, send_sem=send, recv_sem=recv,
            device_id=who, device_id_type=MESH,
        )

    def send0(u, which, slot, who, half):
        return remote(
            bbuf.at[home_slot, half] if is_rhs(u) else inputs[u].at[0, half],
            place0(slot, u, half),
            sem_send0.at[which, u, half],
            sem_buf.at[slot, u, half],
            who,
        )

    def over_y(u, half):
        who = {"chain": jnp.where(inner, twin["chain"], across["chain"])}
        return send0(u, 0, jnp.where(inner, 0, 1 + a), who, half)

    def to_mate(u, half):
        return send0(u, 1, 2 - a, mate, half)

    def start_mate(u):
        for half in range(2):
            to_mate(u, half).start()

    def start_y(u):
        for half in range(2):
            over_y(u, half).start()

    @pl.when(inner)
    def _():
        start_mate(0)
        start_mate(1)

    @pl.when(a == 1)
    def _():
        start_y(0)
        start_y(1)

    @pl.when(a == 0)
    def _():
        start_y(1)
        start_y(0)

    for half in range(2):
        for part in range(2):
            load_rhs(half, part).wait()
    start_y(RHS)
    pl.when(inner)(lambda: start_mate(RHS))

    def hand_on(half):
        return remote(
            bbuf.at[0, half], fwd.at[half], sem_fwd.at[0, half], sem_fwd.at[1, half], pass_on
        )

    def hand_across(half):
        return remote(
            fwd.at[half], bbuf.at[2 - a, half], sem_fwd.at[2, half],
            sem_buf.at[2 - a, RHS, half], diag,
        )

    @pl.when(has_pass_on)
    def _():
        for half in range(2):
            hand_on(half).start()

    none_far0 = outer & jnp.logical_not(has_far)

    def clear(ref):
        ref[...] = jnp.zeros(ref.shape, ref.dtype)

    @pl.when(none_far0)
    def _():
        clear(buf.at[1 + a])
        clear(bbuf.at[1 + a])

    @pl.when(jnp.logical_not(has_down1))
    def _():
        clear(got1.at[0])
        clear(gb1.at[0])

    @pl.when(jnp.logical_not(has_up1))
    def _():
        clear(got1.at[1])
        clear(gb1.at[1])

    @pl.when(jnp.logical_not(has_down2))
    def _():
        clear(got2.at[0])
        clear(gb2.at[0])

    @pl.when(jnp.logical_not(has_up2))
    def _():
        clear(got2.at[1])
        clear(gb2.at[1])

    def arrive(ref, sem):
        pltpu.make_async_copy(ref, ref, sem).wait()

    for u in (0, 1):
        load(u).wait()

    def relay(u, half):
        return remote(
            place0(2 - a, u, half),
            place0(1 + a, u, half),
            sem_relay.at[u, half],
            sem_buf.at[1 + a, u, half],
            far,
        )

    def wait_half(u, half):
        arrive(place0(2 - a, u, half), sem_buf.at[2 - a, u, half])
        if not is_rhs(u):
            pl.when(inner & has_far)(lambda: relay(u, half).start())

    def wait_own(u, half):
        pl.when(inner)(lambda: arrive(place0(0, u, half), sem_buf.at[0, u, half]))

    def wait_unit(u):
        for half in range(2):
            wait_half(u, half)
        for half in range(2):
            wait_own(u, half)

    def wait_far(u, half):
        pl.when(outer & has_far)(
            lambda: arrive(place0(1 + a, u, half), sem_buf.at[1 + a, u, half])
        )

    row = lax.broadcasted_iota(jnp.int32, (l_ref.shape[2], l_ref.shape[3]), 0)
    col = lax.broadcasted_iota(jnp.int32, (l_ref.shape[2], l_ref.shape[3]), 1)
    unit = (row == col).astype(jnp.float32)

    def inverse(off):
        low = rounded((unit - off[0], -off[1]))
        approx = rounded((unit + off[0], off[1]))
        for _ in range(2):
            prod = product(low, approx)
            fix = rounded((2.0 * unit - prod[0], -prod[1]))
            approx = rounded(product(approx, fix))
        return approx

    def negated(parts):
        return -parts[0], -parts[1]

    def coupled(one, two):
        return one[0] + two[0], one[1] + two[1]

    def by_rhs(left, right):
        order = left.shape[1]
        tall = left.reshape(2 * order, left.shape[2])
        both = jnp.dot(tall, right, preferred_element_type=jnp.float32)
        top, low = both[:order], both[order:]
        return jnp.concatenate(
            [top[:, :wide] - low[:, wide:], top[:, wide:] + low[:, :wide]], axis=1
        )

    def new_rhs(inv, own, one, two):
        return by_rhs(
            inv, (own.astype(jnp.float32) - one - two).astype(jnp.bfloat16)
        ).astype(jnp.bfloat16)

    def send1(u, to_up):
        side = 0 if to_up else 1
        rhs = is_rhs(u)
        return remote(
            nb1.at[u - RHS] if rhs else new1.at[u],
            gb1.at[side, u - RHS] if rhs else got1.at[side, u],
            sem_send1.at[side, u],
            sem_got1.at[side, u],
            up1 if to_up else down1,
        )

    def start1(u):
        pl.when(has_up1)(lambda: send1(u, True).start())
        pl.when(has_down1)(lambda: send1(u, False).start())

    wait_unit(f)
    mid[0] = rounded(negated(product(buf[0, f], buf[cf, f])))

    @pl.when(outer & has_far_in)
    def _():
        for half in range(2):
            arrive(fwd.at[half], sem_fwd.at[1, half])
            hand_across(half).start()

    wait_unit(g)
    for half in range(2):
        wait_far(f, half)
    mid[2] = inverse(
        coupled(product(buf[0, f], buf[cf, g]), product(buf[0, g], buf[cg, f]))
    )
    new1[f] = rounded(product(mid[2], mid[0]))
    start1(f)
    for half in range(2):
        wait_far(g, half)
    mid[1] = rounded(negated(product(buf[0, g], buf[cg, g])))
    new1[g] = rounded(product(mid[2], mid[1]))
    start1(g)
    for half in range(2):
        wait_half(RHS, half)
        wait_own(RHS, half)
        wait_far(RHS, half)
        one = by_rhs(buf[0, f], bbuf[cf, half])
        two = by_rhs(buf[0, g], bbuf[cg, half])
        nb1[half] = new_rhs(mid[2], bbuf[0, half], one, two)
        start1(RHS + half)

    def wait1(u):
        rhs = is_rhs(u)

        def one_side(side):
            arrive(gb1.at[side, u - RHS] if rhs else got1.at[side, u], sem_got1.at[side, u])

        pl.when(has_down1)(lambda: one_side(0))
        pl.when(has_up1)(lambda: one_side(1))

    def send2(place, to_up):
        side = 0 if to_up else 1
        return remote(
            new2.at[1 - side] if place == 0 else nb2.at[place - 1],
            got2.at[side] if place == 0 else gb2.at[side, place - 1],
            sem_send2.at[side, place],
            sem_got2.at[side, place],
            up2 if to_up else down2,
        )

    ef, eg = cf - 1, cg - 1
    wait1(f)
    mid[0] = rounded(negated(product(new1[f], got1[ef, f])))
    wait1(g)
    mid[2] = inverse(
        coupled(product(new1[f], got1[ef, g]), product(new1[g], got1[eg, f]))
    )
    new2[f] = rounded(product(mid[2], mid[0]))

    def start2(is_upper):
        pl.when(has_up2 & is_upper)(lambda: send2(0, True).start())
        pl.when(has_down2 & jnp.logical_not(is_upper))(lambda: send2(0, False).start())

    start2(f == 1)
    mid[1] = rounded(negated(product(new1[g], got1[eg, g])))
    new2[g] = rounded(product(mid[2], mid[1]))
    start2(g == 1)
    for half in range(2):
        wait1(RHS + half)
        one = by_rhs(new1[f], gb1[ef, half])
        two = by_rhs(new1[g], gb1[eg, half])
        nb2[half] = new_rhs(mid[2], nb1[half], one, two)
        pl.when(has_up2)(lambda half=half: send2(1 + half, True).start())
        pl.when(has_down2)(lambda half=half: send2(1 + half, False).start())

    def wait2(place):
        def one_side(side):
            arrive(got2.at[side] if place == 0 else gb2.at[side, place - 1], sem_got2.at[side, place])

        pl.when(has_down2)(lambda: one_side(0))
        pl.when(has_up2)(lambda: one_side(1))

    def spot(half, part):
        return (
            last.at[half, :, pl.ds(part * wide, wide)],
            out_ref.at[0, part, :, pl.ds(half * wide, wide)],
        )

    def home(half, part):
        src, dst = spot(half, part)
        return remote(src, dst, sem_out.at[0, half, part], sem_out.at[1, half, part], twin)

    def keep(half, part):
        src, dst = spot(half, part)
        return pltpu.make_async_copy(src, dst, sem_out.at[1, half, part])

    wait2(0)
    mid[2] = inverse(coupled(product(new2[0], got2[0]), product(new2[1], got2[1])))
    for half in range(2):
        wait2(1 + half)
        one = by_rhs(new2[0], gb2[0, half])
        two = by_rhs(new2[1], gb2[1, half])
        last[half] = new_rhs(mid[2], nb2[half], one, two)
        for part in range(2):
            pl.when(inner)(lambda half=half, part=part: home(half, part).start())
            pl.when(outer)(lambda half=half, part=part: keep(half, part).start())

    for u in range(3):
        for half in range(2):
            over_y(u, half).wait_send()
            pl.when(inner)(lambda u=u, half=half: to_mate(u, half).wait_send())
            if u != RHS:
                pl.when(inner & has_far)(lambda u=u, half=half: relay(u, half).wait_send())
    for half in range(2):
        pl.when(has_pass_on)(lambda half=half: hand_on(half).wait_send())
        pl.when(outer & has_far_in)(lambda half=half: hand_across(half).wait_send())
    for u in range(4):
        pl.when(has_up1)(lambda u=u: send1(u, True).wait_send())
        pl.when(has_down1)(lambda u=u: send1(u, False).wait_send())
    for place in range(3):
        pl.when(has_up2)(lambda place=place: send2(place, True).wait_send())
        pl.when(has_down2)(lambda place=place: send2(place, False).wait_send())
    for half in range(2):
        for part in range(2):
            pl.when(inner)(lambda half=half, part=part: home(half, part).wait())
            pl.when(outer)(lambda half=half, part=part: keep(half, part).wait())


def local(quads, lower, upper, right_side):
    block = lower.shape[1:]
    half = (right_side.shape[2], right_side.shape[3])
    any_spec = pl.BlockSpec(memory_space=pl.ANY)
    low = jnp.bfloat16
    dma = pltpu.SemaphoreType.DMA
    return pl.pallas_call(
        functools.partial(kernel, quads),
        out_shape=jax.ShapeDtypeStruct(right_side.shape, right_side.dtype),
        in_specs=[any_spec] * 3,
        out_specs=any_spec,
        scratch_shapes=[
            pltpu.VMEM((3, 2, *block), low),
            pltpu.VMEM((3, 2, *half), low),
            pltpu.VMEM((2, *block), low),
            pltpu.VMEM((2, *half), low),
            pltpu.VMEM((2, 2, *block), low),
            pltpu.VMEM((2, 2, *half), low),
            pltpu.VMEM((2, *block), low),
            pltpu.VMEM((2, *half), low),
            pltpu.VMEM((2, *block), low),
            pltpu.VMEM((2, 2, *half), low),
            pltpu.VMEM((2, *half), low),
            pltpu.VMEM((3, *block), low),
            pltpu.VMEM((2, *half), low),
            dma((2,)),
            dma((2, 2)),
            dma((3, 3, 2)),
            dma((2, 3, 2)),
            dma((3, 2)),
            dma((2, 4)),
            dma((2, 4)),
            dma((2, 3)),
            dma((2, 3)),
            dma((2, 2, 2)),
            dma((3, 2)),
        ],
        compiler_params=pltpu.CompilerParams(collective_id=0, has_side_effects=True),
    )(lower, upper, right_side)


def solution(mesh):
    placed = P(("energy", "chain"), None, None, None)
    return jax.shard_map(
        functools.partial(local, mesh.shape["chain"] // 4),
        mesh=mesh,
        in_specs=(placed,) * 3,
        out_specs=placed,
        check_vma=False,
    )
```

profile of v0, /device:TPU:1, one launch (start us, length us, event | category | flops | bytes accessed | tf_op | source)
XLA Modules:
  0.0 52.7 jit_solution(16430752991388349735)
XLA Ops:
  0.0 51.1 %shard_map.37 = bf16[1,2,256,256]{3,2,1,0:T(8,128)(2,1)} custom-call(bf16[1,2,256,256]{3,2,1,0:T(8,128)(2,1)} %l_ref.1, bf16[1,2,256,256]{3,2,1,0:T(8,128)(2,1)} %u_ref.1, bf16[1,2,256,256]{3,2,1,0:T(8,128)(2,1)} %b_ref.1), custom_call_target="tpu_custom_call" | custom-call | tf_op jit(solution)/shard_map/pallas_call | solution.py:417
  51.1 1.7 %copy.5 = bf16[1,2,256,256]{3,2,1,0:T(8,128)(2,1)} copy(bf16[1,2,256,256]{3,2,1,0:T(8,128)(2,1)} %shard_map.37) | data formatting | bytes 524288
where the time goes:
time: 53.1 us; the launch traced here: 52.7 us
  Pallas kernels  51.1 us (96%)
  local copies, waits for them, and re-layouts  1.67 us (3%)
    pallas_call x1, Pallas kernels, local(): pl.pallas_call(functools.partial(kernel, quads), out_shape=jax.ShapeDtype...  51.1 us
    unnamed x1, local copies, waits for them, and re-layouts  1.67 us

commit v1 on v0

v1 whole, which is shorter than its diff:
```python
import functools

import jax
import jax.numpy as jnp
from jax import lax
from jax.experimental import pallas as pl
from jax.experimental.pallas import tpu as pltpu
from jax.sharding import PartitionSpec as P

NS_STEPS = 2
MESH = pl.DeviceIdType.MESH
LOW = jnp.bfloat16

F, K = 0, 1
OWN, FW, BW = 0, 1, 2


def dot(left, right):
    return jnp.dot(left, right, preferred_element_type=jnp.float32)


def product(*pairs):
    left = jnp.concatenate([part for l, _ in pairs for part in (l[0], l[1])], axis=1)
    real = jnp.concatenate([part for _, r in pairs for part in (r[0], -r[1])], axis=0)
    imag = jnp.concatenate([part for _, r in pairs for part in (r[1], r[0])], axis=0)
    return dot(left, real), dot(left, imag)


def rhs_product(*pairs):
    left = jnp.concatenate([part for l, _ in pairs for part in (l[0], l[1])], axis=1)
    right = []
    for _, r in pairs:
        wide = r.shape[1] // 2
        right += [r, jnp.concatenate([-r[:, wide:], r[:, :wide]], axis=1)]
    return dot(left, jnp.concatenate(right, axis=0))


def rounded(parts):
    return jnp.stack([parts[0].astype(LOW), parts[1].astype(LOW)])


def negated(parts):
    return -parts[0], -parts[1]


def kernel(
    quads, l_ref, u_ref, b_ref, out_ref,
    u0, b0, own1, bown1, u1, b1, own2, bown2, u2, b2, last, inv, raw, low, fix,
    sem_load, sem_bload, sem_m, sem_y, sem_d, sem_r,
    sem_1m, sem_1z, sem_1r, sem_2s, sem_2r, sem_out,
):
    me = lax.axis_index("chain")
    q = me // 4
    a = (me // 2) % 2
    b = me % 2
    inner = a != b
    outer = a == b
    qf, qb = q + 1 - 2 * a, q - 1 + 2 * a
    has_fw = (qf >= 0) & (qf < quads)
    has_bw = (qb >= 0) & (qb < quads)
    order = l_ref.shape[2]
    wide = b_ref.shape[3] // 2

    def at(quad, y, core):
        return {"chain": quad * 4 + y * 2 + core}

    mate = at(q, a, 1 - b)
    across = at(q, 1 - a, b)
    twin = at(q, b, a)
    fw, bw = at(qf, a, b), at(qb, a, b)
    side = {"chain": jnp.where(inner, at(qf, a, 1 - b)["chain"], at(qb, a, 1 - b)["chain"])}
    has_side = (inner & has_fw) | (outer & has_bw)
    diag = at(qb, 1 - a, 1 - b)
    has_diag = outer & has_bw

    def local(src, dst, sem):
        return pltpu.make_async_copy(src, dst, sem)

    def remote(src, dst, send, recv, who):
        return pltpu.make_async_remote_copy(
            src_ref=src, dst_ref=dst, send_sem=send, recv_sem=recv,
            device_id=who, device_id_type=MESH,
        )

    def arrive(ref, sem):
        pltpu.make_async_copy(ref, ref, sem).wait()

    def when(condition, action):
        pl.when(condition)(action)

    home = jnp.where(outer, OWN, BW)

    def load(unit):
        place = jnp.where(a == 0, 1 - unit, unit)
        return local((l_ref, u_ref)[unit].at[0], u0.at[home, place], sem_load.at[unit])

    def load_rhs(half, part):
        return local(
            b_ref.at[0, part, :, pl.ds(half * wide, wide)],
            b0.at[home, half, :, pl.ds(part * wide, wide)],
            sem_bload.at[half, part],
        )

    for unit in range(2):
        load(unit).start()
    for half in range(2):
        for part in range(2):
            load_rhs(half, part).start()

    barrier = pltpu.get_barrier_semaphore()

    def greet(who):
        pl.semaphore_signal(barrier, inc=1, device_id=who, device_id_type=MESH)

    greet(mate)
    greet(across)
    greetings = ((has_side, side), (has_diag, diag), (inner, twin), (has_fw, fw), (has_bw, bw))
    count = 2
    for exists, who in greetings:
        when(exists, functools.partial(greet, who))
        count = count + exists.astype(jnp.int32)

    def clear(ref):
        ref[...] = jnp.zeros(ref.shape, ref.dtype)

    has_one = {FW: outer | has_fw, BW: inner | has_bw}
    has_two = {FW: has_fw, BW: has_bw}

    @pl.when(outer & jnp.logical_not(has_bw))
    def _():
        clear(u0.at[BW])
        clear(b0.at[BW])

    for slot in (FW, BW):
        @pl.when(jnp.logical_not(has_one[slot]))
        def _():
            clear(u1.at[slot - 1])
            clear(b1.at[slot - 1])

        @pl.when(jnp.logical_not(has_two[slot]))
        def _():
            clear(u2.at[slot - 1])
            clear(b2.at[slot - 1])

    for unit in range(2):
        load(unit).wait()
    pl.semaphore_wait(barrier, count)

    def to_mate(item):
        if item < 2:
            src, dst = u0.at[BW, item], u0.at[FW, item]
        else:
            src, dst = b0.at[BW, item - 2], b0.at[FW, item - 2]
        return remote(src, dst, sem_m.at[0, item], sem_m.at[1, item], mate)

    def mate_in(item):
        ref = u0.at[FW, item] if item < 2 else b0.at[FW, item - 2]
        arrive(ref, sem_m.at[1, item])

    def y_place(item):
        if item < 8:
            return u0.at[FW if item < 4 else OWN, (item // 2) % 2, item % 2]
        return b0.at[FW if item < 10 else OWN, item % 2]

    def over_y(item):
        if item < 8:
            src = u0.at[OWN if item < 4 else FW, 1 - (item // 2) % 2, item % 2]
        else:
            src = b0.at[OWN if item < 10 else FW, item % 2]
        return remote(src, y_place(item), sem_y.at[0, item], sem_y.at[1, item], across)

    def y_in(item):
        arrive(y_place(item), sem_y.at[1, item])

    def relay(item):
        return remote(
            y_place(item), u0.at[BW, item // 2, item % 2],
            sem_r.at[0, item], sem_r.at[1, item], side,
        )

    def relay_in(item):
        arrive(u0.at[BW, item // 2, item % 2], sem_r.at[1, item])

    def over_diag(half):
        return remote(
            b0.at[OWN, half], b0.at[BW, half], sem_d.at[0, half], sem_d.at[1, half], diag
        )

    def wait_rhs():
        for half in range(2):
            for part in range(2):
                load_rhs(half, part).wait()

    @pl.when(inner)
    def _():
        to_mate(K).start()
        to_mate(F).start()
        wait_rhs()
        for half in range(2):
            to_mate(2 + half).start()
        for item in range(4):
            y_in(item)
            when(has_fw, lambda item=item: relay(item).start())
        for item in (4, 5):
            y_in(item)

    @pl.when(outer)
    def _():
        for item in range(4):
            over_y(item).start()
        mate_in(K)
        for item in (4, 5):
            over_y(item).start()
        mate_in(F)
        for item in (6, 7):
            over_y(item).start()
        wait_rhs()
        for item in (8, 9):
            over_y(item).start()
        for half in range(2):
            mate_in(2 + half)
        for item in (10, 11):
            over_y(item).start()

    row = lax.broadcasted_iota(jnp.int32, (order, order), 0)
    col = lax.broadcasted_iota(jnp.int32, (order, order), 1)
    unit_matrix = (row == col).astype(jnp.float32)

    def inverse(off, number):
        x = inv.at[number]
        low[...] = rounded((unit_matrix - off[0], -off[1]))
        x[...] = rounded((unit_matrix + off[0], off[1]))
        for _ in range(NS_STEPS):
            prod = product((low[...], x[...]))
            fix[...] = rounded((2.0 * unit_matrix - prod[0], -prod[1]))
            x[...] = rounded(product((x[...], fix[...])))

    def new_rhs(number, own, k, f, behind, ahead):
        change = rhs_product((k, behind), (f, ahead))
        residual = (own.astype(jnp.float32) - change).astype(LOW)
        return rhs_product((inv[number], residual)).astype(LOW)

    mate_slot = jnp.where(outer, BW - 1, FW - 1)
    side_slot = jnp.where(outer, FW - 1, BW - 1)

    def send1(item, slot, sem, who):
        if item < 2:
            src, dst = own1.at[item], u1.at[slot, item]
        else:
            src, dst = bown1.at[item - 2], b1.at[slot, item - 2]
        return remote(src, dst, sem.at[item], sem_1r.at[slot, item], who)

    def to_side1(item):
        return send1(item, side_slot, sem_1z, side)

    def to_mate1(item):
        return send1(item, mate_slot, sem_1m, mate)

    def start1(item):
        when(has_side, lambda: to_side1(item).start())
        to_mate1(item).start()

    def in1(slot, item):
        ref = u1.at[slot - 1, item] if item < 2 else b1.at[slot - 1, item - 2]
        when(has_one[slot], lambda: arrive(ref, sem_1r.at[slot - 1, item]))

    def send2(item, ahead):
        slot = (BW if ahead else FW) - 1
        if item == 0:
            src, dst = own2.at[F if ahead else K], u2.at[slot]
        else:
            src, dst = bown2.at[item - 1], b2.at[slot, item - 1]
        way = 0 if ahead else 1
        return remote(
            src, dst, sem_2s.at[way, item], sem_2r.at[slot, item], fw if ahead else bw
        )

    def start2(item, ahead):
        when(has_fw if ahead else has_bw, lambda: send2(item, ahead).start())

    def in2(slot, item):
        ref = u2.at[slot - 1] if item == 0 else b2.at[slot - 1, item - 1]
        when(has_two[slot], lambda: arrive(ref, sem_2r.at[slot - 1, item]))

    raw[F] = rounded(negated(product((u0[OWN, F], u0[FW, F]))))

    @pl.when(inner)
    def _():
        for item in (6, 7):
            y_in(item)

    @pl.when(has_diag)
    def _():
        for item in (0, 1):
            relay_in(item)

    inverse(product((u0[OWN, K], u0[BW, F]), (u0[OWN, F], u0[FW, K])), 0)
    own1[F] = rounded(product((inv[0], raw[F])))
    start1(F)

    @pl.when(has_diag)
    def _():
        for item in (2, 3):
            relay_in(item)

    raw[K] = rounded(negated(product((u0[OWN, K], u0[BW, K]))))
    own1[K] = rounded(product((inv[0], raw[K])))
    start1(K)

    def rhs0():
        for half in range(2):
            @pl.when(inner)
            def _():
                y_in(8 + half)
                y_in(10 + half)

            when(has_diag, lambda: arrive(b0.at[BW, half], sem_d.at[1, half]))
            bown1[half] = new_rhs(
                0, b0[OWN, half], u0[OWN, K], u0[OWN, F], b0[BW, half], b0[FW, half]
            )
            start1(2 + half)

    @pl.when(outer)
    def _():
        for item in (6, 7):
            over_y(item).wait_send()
        for half in range(2):
            when(has_bw, lambda half=half: over_diag(half).start())
        rhs0()

    in1(FW, K)
    in1(BW, F)
    inverse(product((own1[K], u1[BW - 1, F]), (own1[F], u1[FW - 1, K])), 1)

    def factor1(unit):
        slot = FW if unit == F else BW
        in1(slot, unit)
        raw[unit] = rounded(negated(product((own1[unit], u1[slot - 1, unit]))))
        own2[unit] = rounded(product((inv[1], raw[unit])))
        start2(0, unit == F)

    @pl.when(outer)
    def _():
        factor1(F)
        factor1(K)

    @pl.when(inner)
    def _():
        factor1(K)
        factor1(F)
        rhs0()

    for half in range(2):
        in1(FW, 2 + half)
        in1(BW, 2 + half)
        bown2[half] = new_rhs(
            1, bown1[half], own1[K], own1[F], b1[BW - 1, half], b1[FW - 1, half]
        )
        start2(1 + half, True)
        start2(1 + half, False)

    def spot(half, part):
        return (
            last.at[half, :, pl.ds(part * wide, wide)],
            out_ref.at[0, part, :, pl.ds(half * wide, wide)],
        )

    def give(half, part):
        src, dst = spot(half, part)
        return remote(src, dst, sem_out.at[0, half, part], sem_out.at[1, half, part], twin)

    def keep(half, part):
        src, dst = spot(half, part)
        return local(src, dst, sem_out.at[1, half, part])

    in2(FW, 0)
    in2(BW, 0)
    inverse(product((own2[K], u2[BW - 1]), (own2[F], u2[FW - 1])), 2)
    for half in range(2):
        in2(FW, 1 + half)
        in2(BW, 1 + half)
        last[half] = new_rhs(
            2, bown2[half], own2[K], own2[F], b2[BW - 1, half], b2[FW - 1, half]
        )
        for part in range(2):
            when(inner, lambda half=half, part=part: give(half, part).start())
            when(outer, lambda half=half, part=part: keep(half, part).start())

    @pl.when(inner)
    def _():
        for item in range(4):
            to_mate(item).wait_send()
            when(has_fw, lambda item=item: relay(item).wait_send())

    @pl.when(outer)
    def _():
        for item in range(12):
            if item not in (6, 7):
                over_y(item).wait_send()
        for half in range(2):
            when(has_bw, lambda half=half: over_diag(half).wait_send())

    for item in range(4):
        when(has_side, lambda item=item: to_side1(item).wait_send())
        to_mate1(item).wait_send()
    for item in range(3):
        when(has_fw, lambda item=item: send2(item, True).wait_send())
        when(has_bw, lambda item=item: send2(item, False).wait_send())
    for half in range(2):
        for part in range(2):
            when(inner, lambda half=half, part=part: give(half, part).wait())
            when(outer, lambda half=half, part=part: keep(half, part).wait())


def local_call(quads, lower, upper, right_side):
    block = lower.shape[1:]
    half = (right_side.shape[2], right_side.shape[3])
    anywhere = pl.BlockSpec(memory_space=pl.ANY)
    dma = pltpu.SemaphoreType.DMA
    vmem = lambda *shape: pltpu.VMEM(shape, LOW)
    return pl.pallas_call(
        functools.partial(kernel, quads),
        out_shape=jax.ShapeDtypeStruct(right_side.shape, right_side.dtype),
        in_specs=[anywhere] * 3,
        out_specs=anywhere,
        scratch_shapes=[
            vmem(3, 2, *block),
            vmem(3, 2, *half),
            vmem(2, *block),
            vmem(2, *half),
            vmem(2, 2, *block),
            vmem(2, 2, *half),
            vmem(2, *block),
            vmem(2, *half),
            vmem(2, *block),
            vmem(2, 2, *half),
            vmem(2, *half),
            vmem(3, *block),
            vmem(2, *block),
            vmem(*block),
            vmem(*block),
            dma((2,)),
            dma((2, 2)),
            dma((2, 4)),
            dma((2, 12)),
            dma((2, 2)),
            dma((2, 4)),
            dma((4,)),
            dma((4,)),
            dma((2, 4)),
            dma((2, 3)),
            dma((2, 3)),
            dma((2, 2, 2)),
        ],
        compiler_params=pltpu.CompilerParams(collective_id=0, has_side_effects=True),
    )(lower, upper, right_side)


def solution(mesh):
    placed = P(("energy", "chain"), None, None, None)
    return jax.shard_map(
        functools.partial(local_call, mesh.shape["chain"] // 4),
        mesh=mesh,
        in_specs=(placed,) * 3,
        out_specs=placed,
        check_vma=False,
    )
```

time: 53.1 us -> 48.2 us (0.908)
  Pallas kernels: 51.1 us -> 46.4 us
    pallas_call x1, Pallas kernels: 51.1 us -> 46.4 us  [local_call(): pl.pallas_call(functools.partial(kernel, quads), out_shape=jax.ShapeDtype...]
where the time goes in v1:
time: 48.2 us; the launch traced here: 48.1 us
  Pallas kernels  46.4 us (96%)
  local copies, waits for them, and re-layouts  1.67 us (3%)
    pallas_call x1, Pallas kernels, local_call(): pl.pallas_call(functools.partial(kernel, quads), out_shape=jax.ShapeDtype...  46.4 us
    unnamed x1, local copies, waits for them, and re-layouts  1.67 us

profile of v1, /device:TPU:1, one launch (start us, length us, event | category | flops | bytes accessed | tf_op | source)
XLA Modules:
  0.0 48.1 jit_solution(7031718086473058347)
XLA Ops:
  0.0 46.4 %shard_map.37 = bf16[1,2,256,256]{3,2,1,0:T(8,128)(2,1)} custom-call(bf16[1,2,256,256]{3,2,1,0:T(8,128)(2,1)} %l_ref.1, bf16[1,2,256,256]{3,2,1,0:T(8,128)(2,1)} %u_ref.1, bf16[1,2,256,256]{3,2,1,0:T(8,128)(2,1)} %b_ref.1), custom_call_target="tpu_custom_call" | custom-call | tf_op jit(solution)/shard_map/pallas_call | solution.py:421
  46.4 1.7 %copy.5 = bf16[1,2,256,256]{3,2,1,0:T(8,128)(2,1)} copy(bf16[1,2,256,256]{3,2,1,0:T(8,128)(2,1)} %shard_map.37) | data formatting | bytes 524288

commit v2 on v1

--- a/solution.py
+++ b/solution.py
@@ -13,6 +13,7 @@
 
 F, K = 0, 1
 OWN, FW, BW = 0, 1, 2
+SOWN, SFAR = 3, 4
 
 
 def dot(left, right):
@@ -45,8 +46,8 @@
 
 def kernel(
     quads, l_ref, u_ref, b_ref, out_ref,
-    u0, b0, own1, bown1, u1, b1, own2, bown2, u2, b2, last, inv, raw, low, fix,
-    sem_load, sem_bload, sem_m, sem_y, sem_d, sem_r,
+    u0, b0, own1, bown1, u1, b1, own2, bown2, u2, b2, last, inv, raw, side_raw, low, fix,
+    sem_load, sem_bload, sem_m, sem_y, sem_d, sem_s,
     sem_1m, sem_1z, sem_1r, sem_2s, sem_2r, sem_out,
 ):
     me = lax.axis_index("chain")
@@ -131,10 +132,14 @@
         clear(u0.at[BW])
         clear(b0.at[BW])
 
+    @pl.when(jnp.logical_not(has_side))
+    def _():
+        clear(u0.at[SOWN])
+        clear(u0.at[SFAR])
+
     for slot in (FW, BW):
         @pl.when(jnp.logical_not(has_one[slot]))
         def _():
-            clear(u1.at[slot - 1])
             clear(b1.at[slot - 1])
 
         @pl.when(jnp.logical_not(has_two[slot]))
@@ -172,14 +177,25 @@
     def y_in(item):
         arrive(y_place(item), sem_y.at[1, item])
 
-    def relay(item):
+    def to_side(source, place, unit, part):
         return remote(
-            y_place(item), u0.at[BW, item // 2, item % 2],
-            sem_r.at[0, item], sem_r.at[1, item], side,
-        )
-
-    def relay_in(item):
-        arrive(u0.at[BW, item // 2, item % 2], sem_r.at[1, item])
+            u0.at[source, unit, part], u0.at[place, unit, part],
+            sem_s.at[0, place - BW, unit, part], sem_s.at[1, place - BW, unit, part], side,
+        )
+
+    def start_side(source, place, unit):
+        for part in range(2):
+            when(has_side, lambda part=part: to_side(source, place, unit, part).start())
+
+    def side_in(place, unit):
+        for part in range(2):
+            ref, sem = u0.at[place, unit, part], sem_s.at[1, place - BW, unit, part]
+            when(has_side, lambda ref=ref, sem=sem: arrive(ref, sem))
+
+    def hand_on(item):
+        y_in(item)
+        source, place = (FW, BW) if item < 4 else (OWN, SOWN)
+        when(has_side, lambda: to_side(source, place, (item // 2) % 2, item % 2).start())
 
     def over_diag(half):
         return remote(
@@ -191,49 +207,26 @@
             for part in range(2):
                 load_rhs(half, part).wait()
 
-    @pl.when(inner)
-    def _():
-        to_mate(K).start()
-        to_mate(F).start()
-        wait_rhs()
-        for half in range(2):
-            to_mate(2 + half).start()
-        for item in range(4):
-            y_in(item)
-            when(has_fw, lambda item=item: relay(item).start())
-        for item in (4, 5):
-            y_in(item)
-
-    @pl.when(outer)
-    def _():
-        for item in range(4):
-            over_y(item).start()
-        mate_in(K)
-        for item in (4, 5):
-            over_y(item).start()
-        mate_in(F)
-        for item in (6, 7):
-            over_y(item).start()
-        wait_rhs()
-        for item in (8, 9):
-            over_y(item).start()
-        for half in range(2):
-            mate_in(2 + half)
-        for item in (10, 11):
-            over_y(item).start()
-
     row = lax.broadcasted_iota(jnp.int32, (order, order), 0)
     col = lax.broadcasted_iota(jnp.int32, (order, order), 1)
     unit_matrix = (row == col).astype(jnp.float32)
 
-    def inverse(off, number):
-        x = inv.at[number]
-        low[...] = rounded((unit_matrix - off[0], -off[1]))
-        x[...] = rounded((unit_matrix + off[0], off[1]))
+    def inverse(*jobs):
+        for place, (off, number) in enumerate(jobs):
+            low[place] = rounded((unit_matrix - off[0], -off[1]))
+            inv[number] = rounded((unit_matrix + off[0], off[1]))
         for _ in range(NS_STEPS):
-            prod = product((low[...], x[...]))
-            fix[...] = rounded((2.0 * unit_matrix - prod[0], -prod[1]))
-            x[...] = rounded(product((x[...], fix[...])))
+            for place, (_, number) in enumerate(jobs):
+                prod = product((low[place], inv[number]))
+                fix[place] = rounded((2.0 * unit_matrix - prod[0], -prod[1]))
+            for place, (_, number) in enumerate(jobs):
+                inv[number] = rounded(product((inv[number], fix[place])))
+
+    def crossed(left, right):
+        return rounded(negated(product((left, right))))
+
+    def solved(number, right):
+        return rounded(product((inv[number], right)))
 
     def new_rhs(number, own, k, f, behind, ahead):
         change = rhs_product((k, behind), (f, ahead))
@@ -257,7 +250,8 @@
         return send1(item, mate_slot, sem_1m, mate)
 
     def start1(item):
-        when(has_side, lambda: to_side1(item).start())
+        if item >= 2:
+            when(has_side, lambda: to_side1(item).start())
         to_mate1(item).start()
 
     def in1(slot, item):
@@ -282,31 +276,6 @@
         ref = u2.at[slot - 1] if item == 0 else b2.at[slot - 1, item - 1]
         when(has_two[slot], lambda: arrive(ref, sem_2r.at[slot - 1, item]))
 
-    raw[F] = rounded(negated(product((u0[OWN, F], u0[FW, F]))))
-
-    @pl.when(inner)
-    def _():
-        for item in (6, 7):
-            y_in(item)
-
-    @pl.when(has_diag)
-    def _():
-        for item in (0, 1):
-            relay_in(item)
-
-    inverse(product((u0[OWN, K], u0[BW, F]), (u0[OWN, F], u0[FW, K])), 0)
-    own1[F] = rounded(product((inv[0], raw[F])))
-    start1(F)
-
-    @pl.when(has_diag)
-    def _():
-        for item in (2, 3):
-            relay_in(item)
-
-    raw[K] = rounded(negated(product((u0[OWN, K], u0[BW, K]))))
-    own1[K] = rounded(product((inv[0], raw[K])))
-    start1(K)
-
     def rhs0():
         for half in range(2):
             @pl.when(inner)
@@ -320,35 +289,104 @@
             )
             start1(2 + half)
 
+    def inverse1():
+        inverse((product((own1[K], u1[BW - 1, F]), (own1[F], u1[FW - 1, K])), 1))
+
+    def factor1(unit):
+        slot = FW if unit == F else BW
+        raw[unit] = crossed(own1[unit], u1[slot - 1, unit])
+        own2[unit] = solved(1, raw[unit])
+        start2(0, unit == F)
+
+    @pl.when(inner)
+    def _():
+        to_mate(K).start()
+        to_mate(F).start()
+        start_side(BW, SFAR, F)
+        wait_rhs()
+        for half in range(2):
+            to_mate(2 + half).start()
+        for item in range(4):
+            hand_on(item)
+        side_in(SOWN, K)
+        side_raw[K] = crossed(u0[SOWN, K], u0[FW, K])
+        for item in (4, 5):
+            hand_on(item)
+        raw[F] = crossed(u0[OWN, F], u0[FW, F])
+        side_in(SOWN, F)
+        side_in(SFAR, K)
+        for item in (6, 7):
+            hand_on(item)
+        start_side(BW, SFAR, K)
+        inverse(
+            (product((u0[OWN, K], u0[BW, F]), (u0[OWN, F], u0[FW, K])), 0),
+            (product((u0[SOWN, K], u0[FW, F]), (u0[SOWN, F], u0[SFAR, K])), 3),
+        )
+        raw[K] = crossed(u0[OWN, K], u0[BW, K])
+        own1[F] = solved(0, raw[F])
+        start1(F)
+        own1[K] = solved(0, raw[K])
+        start1(K)
+        u1[FW - 1, K] = solved(3, side_raw[K])
+        side_in(SFAR, F)
+        in1(BW, F)
+        inverse1()
+        side_raw[F] = crossed(u0[SOWN, F], u0[SFAR, F])
+        u1[FW - 1, F] = solved(3, side_raw[F])
+        factor1(F)
+        in1(BW, K)
+        factor1(K)
+        rhs0()
+
     @pl.when(outer)
     def _():
+        for item in range(4):
+            over_y(item).start()
+        start_side(OWN, SOWN, K)
+        start_side(OWN, SOWN, F)
+        mate_in(K)
+        for item in (4, 5):
+            over_y(item).start()
+        start_side(FW, SFAR, K)
+        mate_in(F)
+        for item in (6, 7):
+            over_y(item).start()
+        start_side(FW, SFAR, F)
+        wait_rhs()
+        for item in (8, 9):
+            over_y(item).start()
+        for half in range(2):
+            mate_in(2 + half)
+        for item in (10, 11):
+            over_y(item).start()
+        raw[F] = crossed(u0[OWN, F], u0[FW, F])
+        side_in(BW, F)
+        inverse((product((u0[OWN, K], u0[BW, F]), (u0[OWN, F], u0[FW, K])), 0))
+        own1[F] = solved(0, raw[F])
+        start1(F)
+        side_in(BW, K)
+        raw[K] = crossed(u0[OWN, K], u0[BW, K])
+        own1[K] = solved(0, raw[K])
+        start1(K)
         for item in (6, 7):
             over_y(item).wait_send()
         for half in range(2):
             when(has_bw, lambda half=half: over_diag(half).start())
-        rhs0()
-
-    in1(FW, K)
-    in1(BW, F)
-    inverse(product((own1[K], u1[BW - 1, F]), (own1[F], u1[FW - 1, K])), 1)
-
-    def factor1(unit):
-        slot = FW if unit == F else BW
-        in1(slot, unit)
-        raw[unit] = rounded(negated(product((own1[unit], u1[slot - 1, unit]))))
-        own2[unit] = rounded(product((inv[1], raw[unit])))
-        start2(0, unit == F)
-
-    @pl.when(outer)
-    def _():
-        factor1(F)
-        factor1(K)
-
-    @pl.when(inner)
-    def _():
-        factor1(K)
+        side_in(SOWN, F)
+        side_raw[F] = crossed(u0[SOWN, F], u0[BW, F])
+        side_in(SFAR, F)
+        side_in(SOWN, K)
+        inverse((product((u0[SOWN, K], u0[SFAR, F]), (u0[SOWN, F], u0[BW, K])), 3))
+        u1[BW - 1, F] = solved(3, side_raw[F])
+        in1(FW, F)
+        in1(FW, K)
+        inverse1()
         factor1(F)
         rhs0()
+        side_in(SFAR, K)
+        side_raw[K] = crossed(u0[SOWN, K], u0[SFAR, K])
+        u1[BW - 1, K] = solved(3, side_raw[K])
+        factor1(K)
 
     for half in range(2):
         in1(FW, 2 + half)
@@ -375,7 +413,7 @@
 
     in2(FW, 0)
     in2(BW, 0)
-    inverse(product((own2[K], u2[BW - 1]), (own2[F], u2[FW - 1])), 2)
+    inverse((product((own2[K], u2[BW - 1]), (own2[F], u2[FW - 1])), 2))
     for half in range(2):
         in2(FW, 1 + half)
         in2(BW, 1 + half)
@@ -390,7 +428,6 @@
     def _():
         for item in range(4):
             to_mate(item).wait_send()
-            when(has_fw, lambda item=item: relay(item).wait_send())
 
     @pl.when(outer)
     def _():
@@ -400,8 +437,25 @@
         for half in range(2):
             when(has_bw, lambda half=half: over_diag(half).wait_send())
 
+    def side_sent(source, place):
+        for unit in range(2):
+            for part in range(2):
+                to_side(source, place, unit, part).wait_send()
+
+    @pl.when(inner & has_side)
+    def _():
+        side_sent(FW, BW)
+        side_sent(OWN, SOWN)
+        side_sent(BW, SFAR)
+
+    @pl.when(outer & has_side)
+    def _():
+        side_sent(OWN, SOWN)
+        side_sent(FW, SFAR)
+
     for item in range(4):
-        when(has_side, lambda item=item: to_side1(item).wait_send())
+        if item >= 2:
+            when(has_side, lambda item=item: to_side1(item).wait_send())
         to_mate1(item).wait_send()
     for item in range(3):
         when(has_fw, lambda item=item: send2(item, True).wait_send())
@@ -424,7 +478,7 @@
         in_specs=[anywhere] * 3,
         out_specs=anywhere,
         scratch_shapes=[
-            vmem(3, 2, *block),
+            vmem(5, 2, *block),
             vmem(3, 2, *half),
             vmem(2, *block),
             vmem(2, *half),
@@ -435,16 +489,17 @@
             vmem(2, *block),
             vmem(2, 2, *half),
             vmem(2, *half),
-            vmem(3, *block),
-            vmem(2, *block),
-            vmem(*block),
-            vmem(*block),
+            vmem(4, *block),
+            vmem(2, *block),
+            vmem(2, *block),
+            vmem(2, *block),
+            vmem(2, *block),
             dma((2,)),
             dma((2, 2)),
             dma((2, 4)),
             dma((2, 12)),
             dma((2, 2)),
-            dma((2, 4)),
+            dma((2, 3, 2, 2)),
             dma((4,)),
             dma((4,)),
             dma((2, 4)),

time: 48.2 us -> 45.2 us (0.938)
  Pallas kernels: 46.4 us -> 43.4 us
    pallas_call x1, Pallas kernels: 46.4 us -> 43.4 us  [local_call(): pl.pallas_call(functools.partial(kernel, quads), out_shape=jax.ShapeDtype...]
where the time goes in v2:
time: 45.2 us; the launch traced here: 45 us
  Pallas kernels  43.4 us (96%)
  local copies, waits for them, and re-layouts  1.67 us (4%)
    pallas_call x1, Pallas kernels, local_call(): pl.pallas_call(functools.partial(kernel, quads), out_shape=jax.ShapeDtype...  43.4 us
    unnamed x1, local copies, waits for them, and re-layouts  1.67 us

profile of v2, /device:TPU:1, one launch (start us, length us, event | category | flops | bytes accessed | tf_op | source)
XLA Modules:
  0.0 45.0 jit_solution(1057896093683094283)
XLA Ops:
  0.0 43.4 %shard_map.37 = bf16[1,2,256,256]{3,2,1,0:T(8,128)(2,1)} custom-call(bf16[1,2,256,256]{3,2,1,0:T(8,128)(2,1)} %l_ref.1, bf16[1,2,256,256]{3,2,1,0:T(8,128)(2,1)} %u_ref.1, bf16[1,2,256,256]{3,2,1,0:T(8,128)(2,1)} %b_ref.1), custom_call_target="tpu_custom_call" | custom-call | tf_op jit(solution)/shard_map/pallas_call | solution.py:475
  43.4 1.7 %copy.5 = bf16[1,2,256,256]{3,2,1,0:T(8,128)(2,1)} copy(bf16[1,2,256,256]{3,2,1,0:T(8,128)(2,1)} %shard_map.37) | data formatting | bytes 524288

commit v3 on v2

--- a/solution.py
+++ b/solution.py
@@ -292,11 +292,9 @@
     def inverse1():
         inverse((product((own1[K], u1[BW - 1, F]), (own1[F], u1[FW - 1, K])), 1))
 
-    def factor1(unit):
+    def cross1(unit):
         slot = FW if unit == F else BW
         raw[unit] = crossed(own1[unit], u1[slot - 1, unit])
-        own2[unit] = solved(1, raw[unit])
-        start2(0, unit == F)
 
     @pl.when(inner)
     def _():
@@ -312,30 +310,32 @@
         side_raw[K] = crossed(u0[SOWN, K], u0[FW, K])
         for item in (4, 5):
             hand_on(item)
-        raw[F] = crossed(u0[OWN, F], u0[FW, F])
         side_in(SOWN, F)
         side_in(SFAR, K)
+        inverse((product((u0[SOWN, K], u0[FW, F]), (u0[SOWN, F], u0[SFAR, K])), 3))
+        raw[F] = crossed(u0[OWN, F], u0[FW, F])
+        u1[FW - 1, K] = solved(3, side_raw[K])
         for item in (6, 7):
             hand_on(item)
         start_side(BW, SFAR, K)
-        inverse(
-            (product((u0[OWN, K], u0[BW, F]), (u0[OWN, F], u0[FW, K])), 0),
-            (product((u0[SOWN, K], u0[FW, F]), (u0[SOWN, F], u0[SFAR, K])), 3),
-        )
+        inverse((product((u0[OWN, K], u0[BW, F]), (u0[OWN, F], u0[FW, K])), 0))
         raw[K] = crossed(u0[OWN, K], u0[BW, K])
         own1[F] = solved(0, raw[F])
+        own1[K] = solved(0, raw[K])
         start1(F)
-        own1[K] = solved(0, raw[K])
         start1(K)
-        u1[FW - 1, K] = solved(3, side_raw[K])
         side_in(SFAR, F)
         in1(BW, F)
+        in1(BW, K)
         inverse1()
         side_raw[F] = crossed(u0[SOWN, F], u0[SFAR, F])
         u1[FW - 1, F] = solved(3, side_raw[F])
-        factor1(F)
-        in1(BW, K)
-        factor1(K)
+        for unit in (F, K):
+            cross1(unit)
+        for unit in (F, K):
+            own2[unit] = solved(1, raw[unit])
+        start2(0, True)
+        start2(0, False)
         rhs0()
 
     @pl.when(outer)
@@ -353,12 +353,10 @@
             over_y(item).start()
         start_side(FW, SFAR, F)
         wait_rhs()
-        for item in (8, 9):
-            over_y(item).start()
         for half in range(2):
+            over_y(8 + half).start()
             mate_in(2 + half)
-        for item in (10, 11):
-            over_y(item).start()
+            over_y(10 + half).start()
         raw[F] = crossed(u0[OWN, F], u0[FW, F])
         side_in(BW, F)
         inverse((product((u0[OWN, K], u0[BW, F]), (u0[OWN, F], u0[FW, K])), 0))
@@ -374,19 +372,23 @@
             when(has_bw, lambda half=half: over_diag(half).start())
         side_in(SOWN, F)
         side_raw[F] = crossed(u0[SOWN, F], u0[BW, F])
+        in1(FW, F)
+        in1(FW, K)
+        cross1(F)
         side_in(SFAR, F)
         side_in(SOWN, K)
         inverse((product((u0[SOWN, K], u0[SFAR, F]), (u0[SOWN, F], u0[BW, K])), 3))
         u1[BW - 1, F] = solved(3, side_raw[F])
-        in1(FW, F)
-        in1(FW, K)
         inverse1()
-        factor1(F)
+        own2[F] = solved(1, raw[F])
+        start2(0, True)
         rhs0()
         side_in(SFAR, K)
         side_raw[K] = crossed(u0[SOWN, K], u0[SFAR, K])
         u1[BW - 1, K] = solved(3, side_raw[K])
-        factor1(K)
+        cross1(K)
+        own2[K] = solved(1, raw[K])
+        start2(0, False)
 
     for half in range(2):
         in1(FW, 2 + half)

time: 45.2 us -> 45.1 us (level)
  no operation moved by 1% of the time
where the time goes in v3:
time: 45.1 us; the launch traced here: 45 us
  Pallas kernels  43.3 us (96%)
  local copies, waits for them, and re-layouts  1.67 us (4%)
    pallas_call x1, Pallas kernels, local_call(): pl.pallas_call(functools.partial(kernel, quads), out_shape=jax.ShapeDtype...  43.3 us
    unnamed x1, local copies, waits for them, and re-layouts  1.67 us

profile of v3, /device:TPU:1, one launch (start us, length us, event | category | flops | bytes accessed | tf_op | source)
XLA Modules:
  0.0 45.0 jit_solution(13662920168750564207)
XLA Ops:
  0.0 43.3 %shard_map.37 = bf16[1,2,256,256]{3,2,1,0:T(8,128)(2,1)} custom-call(bf16[1,2,256,256]{3,2,1,0:T(8,128)(2,1)} %l_ref.1, bf16[1,2,256,256]{3,2,1,0:T(8,128)(2,1)} %u_ref.1, bf16[1,2,256,256]{3,2,1,0:T(8,128)(2,1)} %b_ref.1), custom_call_target="tpu_custom_call" | custom-call | tf_op jit(solution)/shard_map/pallas_call | solution.py:477
  43.3 1.7 %copy.5 = bf16[1,2,256,256]{3,2,1,0:T(8,128)(2,1)} copy(bf16[1,2,256,256]{3,2,1,0:T(8,128)(2,1)} %shard_map.37) | data formatting | bytes 524288

commit v4 on v3

--- a/solution.py
+++ b/solution.py
@@ -46,7 +46,7 @@
 
 def kernel(
     quads, l_ref, u_ref, b_ref, out_ref,
-    u0, b0, own1, bown1, u1, b1, own2, bown2, u2, b2, last, inv, raw, side_raw, low, fix,
+    u0, b0, own1, bown1, u1, b1, own2, bown2, u2, b2, last, inv, raw, side_raw, low, fix, partial,
     sem_load, sem_bload, sem_m, sem_y, sem_d, sem_s,
     sem_1m, sem_1z, sem_1r, sem_2s, sem_2r, sem_out,
 ):
@@ -165,13 +165,13 @@
     def y_place(item):
         if item < 8:
             return u0.at[FW if item < 4 else OWN, (item // 2) % 2, item % 2]
-        return b0.at[FW if item < 10 else OWN, item % 2]
+        return b0.at[OWN, item % 2]
 
     def over_y(item):
         if item < 8:
             src = u0.at[OWN if item < 4 else FW, 1 - (item // 2) % 2, item % 2]
         else:
-            src = b0.at[OWN if item < 10 else FW, item % 2]
+            src = partial.at[item % 2]
         return remote(src, y_place(item), sem_y.at[0, item], sem_y.at[1, item], across)
 
     def y_in(item):
@@ -228,10 +228,11 @@
     def solved(number, right):
         return rounded(product((inv[number], right)))
 
-    def new_rhs(number, own, k, f, behind, ahead):
-        change = rhs_product((k, behind), (f, ahead))
-        residual = (own.astype(jnp.float32) - change).astype(LOW)
-        return rhs_product((inv[number], residual)).astype(LOW)
+    def residual(own, *pairs):
+        return (own.astype(jnp.float32) - rhs_product(*pairs)).astype(LOW)
+
+    def new_rhs(number, own, *pairs):
+        return rhs_product((inv[number], residual(own, *pairs))).astype(LOW)
 
     mate_slot = jnp.where(outer, BW - 1, FW - 1)
     side_slot = jnp.where(outer, FW - 1, BW - 1)
@@ -276,18 +277,24 @@
         ref = u2.at[slot - 1] if item == 0 else b2.at[slot - 1, item - 1]
         when(has_two[slot], lambda: arrive(ref, sem_2r.at[slot - 1, item]))
 
-    def rhs0():
-        for half in range(2):
-            @pl.when(inner)
-            def _():
-                y_in(8 + half)
-                y_in(10 + half)
-
-            when(has_diag, lambda: arrive(b0.at[BW, half], sem_d.at[1, half]))
-            bown1[half] = new_rhs(
-                0, b0[OWN, half], u0[OWN, K], u0[OWN, F], b0[BW, half], b0[FW, half]
-            )
-            start1(2 + half)
+    def rhs0(half, *pairs):
+        bown1[half] = new_rhs(0, b0[OWN, half], (u0[OWN, K], b0[BW, half]), *pairs)
+        start1(2 + half)
+
+    def inner_rhs0(half):
+        y_in(8 + half)
+        rhs0(half)
+
+    def outer_rhs0(half):
+        when(has_bw, lambda: arrive(b0.at[BW, half], sem_d.at[1, half]))
+        rhs0(half, (u0[OWN, F], b0[FW, half]))
+
+    def rhs1(half):
+        bown2[half] = new_rhs(
+            1, bown1[half], (own1[K], b1[BW - 1, half]), (own1[F], b1[FW - 1, half])
+        )
+        start2(1 + half, True)
+        start2(1 + half, False)
 
     def inverse1():
         inverse((product((own1[K], u1[BW - 1, F]), (own1[F], u1[FW - 1, K])), 1))
@@ -336,7 +343,12 @@
             own2[unit] = solved(1, raw[unit])
         start2(0, True)
         start2(0, False)
-        rhs0()
+        for half in range(2):
+            inner_rhs0(half)
+        for half in range(2):
+            in1(FW, 2 + half)
+            in1(BW, 2 + half)
+            rhs1(half)
 
     @pl.when(outer)
     def _():
@@ -354,9 +366,8 @@
         start_side(FW, SFAR, F)
         wait_rhs()
         for half in range(2):
-            over_y(8 + half).start()
             mate_in(2 + half)
-            over_y(10 + half).start()
+            partial[half] = residual(b0[FW, half], (u0[FW, K], b0[OWN, half]))
         raw[F] = crossed(u0[OWN, F], u0[FW, F])
         side_in(BW, F)
         inverse((product((u0[OWN, K], u0[BW, F]), (u0[OWN, F], u0[FW, K])), 0))
@@ -370,34 +381,35 @@
             over_y(item).wait_send()
         for half in range(2):
             when(has_bw, lambda half=half: over_diag(half).start())
+        when(has_bw, lambda: over_diag(0).wait_send())
+        for item in (8, 9):
+            over_y(item).start()
         side_in(SOWN, F)
         side_raw[F] = crossed(u0[SOWN, F], u0[BW, F])
         in1(FW, F)
         in1(FW, K)
         cross1(F)
+        outer_rhs0(0)
         side_in(SFAR, F)
         side_in(SOWN, K)
         inverse((product((u0[SOWN, K], u0[SFAR, F]), (u0[SOWN, F], u0[BW, K])), 3))
         u1[BW - 1, F] = solved(3, side_raw[F])
+        outer_rhs0(1)
         inverse1()
         own2[F] = solved(1, raw[F])
-        start2(0, True)
-        rhs0()
         side_in(SFAR, K)
         side_raw[K] = crossed(u0[SOWN, K], u0[SFAR, K])
         u1[BW - 1, K] = solved(3, side_raw[K])
         cross1(K)
         own2[K] = solved(1, raw[K])
         start2(0, False)
-
-    for half in range(2):
-        in1(FW, 2 + half)
-        in1(BW, 2 + half)
-        bown2[half] = new_rhs(
-            1, bown1[half], own1[K], own1[F], b1[BW - 1, half], b1[FW - 1, half]
-        )
-        start2(1 + half, True)
-        start2(1 + half, False)
+        in1(FW, 2)
+        in1(BW, 2)
+        rhs1(0)
+        start2(0, True)
+        in1(FW, 3)
+        in1(BW, 3)
+        rhs1(1)
 
     def spot(half, part):
         return (
@@ -420,7 +432,7 @@
         in2(FW, 1 + half)
         in2(BW, 1 + half)
         last[half] = new_rhs(
-            2, bown2[half], own2[K], own2[F], b2[BW - 1, half], b2[FW - 1, half]
+            2, bown2[half], (own2[K], b2[BW - 1, half]), (own2[F], b2[FW - 1, half])
         )
         for part in range(2):
             when(inner, lambda half=half, part=part: give(half, part).start())
@@ -433,11 +445,10 @@
 
     @pl.when(outer)
     def _():
-        for item in range(12):
+        for item in range(10):
             if item not in (6, 7):
                 over_y(item).wait_send()
-        for half in range(2):
-            when(has_bw, lambda half=half: over_diag(half).wait_send())
+        when(has_bw, lambda: over_diag(1).wait_send())
 
     def side_sent(source, place):
         for unit in range(2):
@@ -496,10 +507,11 @@
             vmem(2, *block),
             vmem(2, *block),
             vmem(2, *block),
+            vmem(2, *half),
             dma((2,)),
             dma((2, 2)),
             dma((2, 4)),
-            dma((2, 12)),
+            dma((2, 10)),
             dma((2, 2)),
             dma((2, 3, 2, 2)),
             dma((4,)),

time: 45.1 us -> 42.1 us (0.933)
  Pallas kernels: 43.3 us -> 40.2 us
    pallas_call x1, Pallas kernels: 43.3 us -> 40.2 us  [local_call(): pl.pallas_call(functools.partial(kernel, quads), out_shape=jax.ShapeDtype...]
where the time goes in v4:
time: 42.1 us; the launch traced here: 41.8 us
  Pallas kernels  40.2 us (95%)
  local copies, waits for them, and re-layouts  1.67 us (4%)
    pallas_call x1, Pallas kernels, local_call(): pl.pallas_call(functools.partial(kernel, quads), out_shape=jax.ShapeDtype...  40.2 us
    unnamed x1, local copies, waits for them, and re-layouts  1.67 us

profile of v4, /device:TPU:1, one launch (start us, length us, event | category | flops | bytes accessed | tf_op | source)
XLA Modules:
  0.0 41.8 jit_solution(9266273100440670891)
XLA Ops:
  0.0 40.2 %shard_map.37 = bf16[1,2,256,256]{3,2,1,0:T(8,128)(2,1)} custom-call(bf16[1,2,256,256]{3,2,1,0:T(8,128)(2,1)} %l_ref.1, bf16[1,2,256,256]{3,2,1,0:T(8,128)(2,1)} %u_ref.1, bf16[1,2,256,256]{3,2,1,0:T(8,128)(2,1)} %b_ref.1), custom_call_target="tpu_custom_call" | custom-call | tf_op jit(solution)/shard_map/pallas_call | solution.py:488
  40.2 1.7 %copy.5 = bf16[1,2,256,256]{3,2,1,0:T(8,128)(2,1)} copy(bf16[1,2,256,256]{3,2,1,0:T(8,128)(2,1)} %shard_map.37) | data formatting | bytes 524288

commit v5 on v4

--- a/solution.py
+++ b/solution.py
@@ -339,10 +339,8 @@
         u1[FW - 1, F] = solved(3, side_raw[F])
         for unit in (F, K):
             cross1(unit)
-        for unit in (F, K):
             own2[unit] = solved(1, raw[unit])
-        start2(0, True)
-        start2(0, False)
+            start2(0, unit == F)
         for half in range(2):
             inner_rhs0(half)
         for half in range(2):
@@ -421,22 +419,28 @@
         src, dst = spot(half, part)
         return remote(src, dst, sem_out.at[0, half, part], sem_out.at[1, half, part], twin)
 
-    def keep(half, part):
-        src, dst = spot(half, part)
-        return local(src, dst, sem_out.at[1, half, part])
-
     in2(FW, 0)
     in2(BW, 0)
     inverse((product((own2[K], u2[BW - 1]), (own2[F], u2[FW - 1])), 2))
     for half in range(2):
         in2(FW, 1 + half)
         in2(BW, 1 + half)
-        last[half] = new_rhs(
+        rows = new_rhs(
             2, bown2[half], (own2[K], b2[BW - 1, half]), (own2[F], b2[FW - 1, half])
         )
-        for part in range(2):
-            when(inner, lambda half=half, part=part: give(half, part).start())
-            when(outer, lambda half=half, part=part: keep(half, part).start())
+
+        @pl.when(inner)
+        def _():
+            last[half] = rows
+            for part in range(2):
+                give(half, part).start()
+
+        @pl.when(outer)
+        def _():
+            for part in range(2):
+                out_ref[0, part, :, half * wide : (half + 1) * wide] = rows[
+                    :, part * wide : (part + 1) * wide
+                ]
 
     @pl.when(inner)
     def _():
@@ -476,7 +480,6 @@
     for half in range(2):
         for part in range(2):
             when(inner, lambda half=half, part=part: give(half, part).wait())
-            when(outer, lambda half=half, part=part: keep(half, part).wait())
 
 
 def local_call(quads, lower, upper, right_side):
@@ -487,9 +490,9 @@
     vmem = lambda *shape: pltpu.VMEM(shape, LOW)
     return pl.pallas_call(
         functools.partial(kernel, quads),
-        out_shape=jax.ShapeDtypeStruct(right_side.shape, right_side.dtype),
+        out_shape=pltpu.VMEM(right_side.shape, right_side.dtype),
         in_specs=[anywhere] * 3,
-        out_specs=anywhere,
+        out_specs=pl.BlockSpec(memory_space=pltpu.VMEM),
         scratch_shapes=[
             vmem(5, 2, *block),
             vmem(3, 2, *half),

time: 42.1 us -> 41 us (0.974)
  local copies, waits for them, and re-layouts: 1.67 us -> 0.71 us
    unnamed x1, local copies, waits for them, and re-layouts: 1.67 us -> 0.71 us
where the time goes in v5:
time: 41 us; the launch traced here: 40.8 us
  Pallas kernels  40.1 us (98%)
  local copies, waits for them, and re-layouts  0.71 us (2%)
    pallas_call x1, Pallas kernels, local_call(): pl.pallas_call(functools.partial(kernel, quads), out_shape=pltpu.VMEM(rig...  40.1 us

profile of v5, /device:TPU:1, one launch (start us, length us, event | category | flops | bytes accessed | tf_op | source)
XLA Modules:
  0.0 40.8 jit_solution(8008671391721737626)
XLA Ops:
  0.0 40.1 %shard_map.37 = bf16[1,2,256,256]{3,2,1,0:T(8,128)(2,1)S(1)} custom-call(bf16[1,2,256,256]{3,2,1,0:T(8,128)(2,1)} %l_ref.1, bf16[1,2,256,256]{3,2,1,0:T(8,128)(2,1)} %u_ref.1, bf16[1,2,256,256]{3,2,1,0:T(8,128)(2,1)} %b_ref.1), custom_call_target="tpu_custom_call" | custom-call | tf_op jit(solution)/shard_map/pallas_call | solution.py:491
  40.1 0.7 %copy.5 = bf16[1,2,256,256]{3,2,1,0:T(8,128)(2,1)} copy(bf16[1,2,256,256]{3,2,1,0:T(8,128)(2,1)S(1)} %shard_map.37) | data formatting | bytes 524288

commit v6 on v5

--- a/solution.py
+++ b/solution.py
@@ -102,12 +102,6 @@
             sem_bload.at[half, part],
         )
 
-    for unit in range(2):
-        load(unit).start()
-    for half in range(2):
-        for part in range(2):
-            load_rhs(half, part).start()
-
     barrier = pltpu.get_barrier_semaphore()
 
     def greet(who):
@@ -120,6 +114,12 @@
     for exists, who in greetings:
         when(exists, functools.partial(greet, who))
         count = count + exists.astype(jnp.int32)
+
+    for unit in range(2):
+        load(unit).start()
+    for half in range(2):
+        for part in range(2):
+            load_rhs(half, part).start()
 
     def clear(ref):
         ref[...] = jnp.zeros(ref.shape, ref.dtype)

time: 41 us -> 41 us (level)
  no operation moved by 1% of the time
where the time goes in v6:
time: 41 us; the launch traced here: 40.7 us
  Pallas kernels  40 us (98%)
  local copies, waits for them, and re-layouts  0.71 us (2%)
    pallas_call x1, Pallas kernels, local_call(): pl.pallas_call(functools.partial(kernel, quads), out_shape=pltpu.VMEM(rig...  40 us

profile of v6, /device:TPU:1, one launch (start us, length us, event | category | flops | bytes accessed | tf_op | source)
XLA Modules:
  0.0 40.7 jit_solution(1804780462579986520)
XLA Ops:
  0.0 40.0 %shard_map.37 = bf16[1,2,256,256]{3,2,1,0:T(8,128)(2,1)S(1)} custom-call(bf16[1,2,256,256]{3,2,1,0:T(8,128)(2,1)} %l_ref.1, bf16[1,2,256,256]{3,2,1,0:T(8,128)(2,1)} %u_ref.1, bf16[1,2,256,256]{3,2,1,0:T(8,128)(2,1)} %b_ref.1), custom_call_target="tpu_custom_call" | custom-call | tf_op jit(solution)/shard_map/pallas_call | solution.py:491
  40.0 0.7 %copy.5 = bf16[1,2,256,256]{3,2,1,0:T(8,128)(2,1)} copy(bf16[1,2,256,256]{3,2,1,0:T(8,128)(2,1)S(1)} %shard_map.37) | data formatting | bytes 524288
